TPU v7x, 32 devices: a whole 2x2x4 slice. The times are simulated.
32 devices in a mesh: dp: 8 (over z, core), mp: 4 (over y, x).
Axes of the slice: x: 2, y: 2, z: 4, core: 2. Of those that a mesh axis runs over, the one named last changes fastest.
Arguments:
- momentum: float32 [8, 256, 5120], P('dp', 'mp'), may hold values from -60 to 60
- gradient: bfloat16 [8, 256, 5120], P('dp', 'mp'), may hold values from -60 to 60
- columns: int32 [256], replicated, may hold values from 0 to 5119, as said below
Outputs:
- update: bfloat16 [256, 5120], P('mp', 'dp')
- new_momentum: float32 [8, 256, 5120], P('dp', 'mp')
Inputs may be any that keep to these rules, and one draw needn't show every extreme that they name: `columns`: 256 distinct frequencies, 0 and 5119 always among them, in no particular order.
All inputs are finite; a program needn't handle non-finite values.
Results may differ from a plain program's by a relative error of at most 0.007.
Values may be sent and summed in bfloat16 or wider, within the bound.
A program may use at most 64 MiB of HBM per device.

v0:
```python
import math

import jax
import jax.numpy as jnp
from jax import lax
from jax.sharding import PartitionSpec as P

COLS = 5120
RANK = 256
ITERS = 5


inertia = 0.9
linear_term = 3.4445
cubic_term = -4.775
quintic_term = 2.0315


def dct_table(columns):
    positions = jnp.arange(COLS, dtype=jnp.int32)
    phase_index = (2 * positions[:, None] + 1) * columns[None, :] % (4 * COLS)
    angles = phase_index.astype(jnp.float32) * (math.pi / (2 * COLS))
    column_scale = jnp.where(columns == 0, math.sqrt(1.0 / COLS), math.sqrt(2.0 / COLS))
    return (jnp.cos(angles) * column_scale[None, :]).astype(jnp.bfloat16)


def orthogonalize(gram_matrix):
    squared_norm = jnp.trace(gram_matrix) + 1e-06
    inverse_norm = 1.0 / jnp.sqrt(squared_norm)
    identity = jnp.eye(gram_matrix.shape[0], dtype=jnp.float32)
    gram_now = gram_matrix * (inverse_norm * inverse_norm)
    mixing = identity * inverse_norm
    highest = lax.Precision.HIGHEST
    for _ in range(ITERS):
        polynomial = (
            linear_term * identity
            + cubic_term * gram_now
            + quintic_term * jnp.dot(gram_now, gram_now, precision=highest)
        )
        mixing = jnp.dot(mixing, polynomial, precision=highest)
        gram_now = jnp.dot(
            jnp.dot(polynomial, gram_now, precision=highest), polynomial, precision=highest
        )
    return mixing


def body(momentum, gradient, columns):
    highest = lax.Precision.HIGHEST
    cosines = dct_table(columns)
    current = inertia * momentum[0] + gradient[0].astype(jnp.float32)
    partial_value = jnp.dot(
        current.astype(jnp.bfloat16), cosines, preferred_element_type=jnp.float32
    )
    replica_count = lax.axis_size("dp")
    summed = lax.psum(partial_value, "dp") / replica_count
    coded_rows = summed.astype(jnp.bfloat16)
    block_rows = lax.all_gather(summed, "mp", axis=0, tiled=True)
    gram_matrix = jnp.dot(block_rows.T, block_rows, precision=highest)
    mixing = orthogonalize(gram_matrix)
    orthogonal = jnp.dot(summed, mixing, precision=highest).astype(jnp.bfloat16)
    decoded = jnp.dot(coded_rows, cosines.T, preferred_element_type=jnp.float32)
    band_width = COLS // replica_count
    band_start = lax.axis_index("dp") * band_width
    band_cosines = lax.dynamic_slice_in_dim(cosines, band_start, band_width, 0)
    direction = jnp.dot(orthogonal, band_cosines.T, preferred_element_type=jnp.float32)
    row_count = momentum.shape[1] * lax.axis_size("mp")
    update = (direction * math.sqrt(row_count * COLS / RANK)).astype(jnp.bfloat16)
    new_momentum = (current - decoded)[None]
    return (update, new_momentum)


def solution(mesh):
    return jax.shard_map(
        body,
        mesh=mesh,
        in_specs=(P("dp", "mp", None), P("dp", "mp", None), P()),
        out_specs=(P("mp", "dp"), P("dp", "mp", None)),
        check_vma=False,
    )
```

profile of v0, /device:TPU:0, one launch (start us, length us, event | category | flops | bytes accessed | tf_op | source)
XLA Modules:
  0.0 141.9 jit_solution(5607261184913191640)
XLA Ops:
  7.2 0.0 all-reduce.2.cloned.1.call-start
  7.2 0.7 compare_select_fusion
  7.9 0.0 copy-start.1
  7.9 25.8 %fusion.15 = f32[64,256]{1,0:T(8,128)} fusion(bf16[1,64,5120]{2,1,0:T(8,128)(2,1)} %param.4, f32[1,64,5120]{2,1,0:T(8,128)} %param.3, f32[256]{0:T(256)S(1)} %compare_select_fusion, s32[256]{0:T(256)} %param.5, s32[5120]{0:T(1024)S(1)} %multiply_add_fusion), kind=kOutput, calls=%fused_computation.27 | convolution fusion | flops 183500800 | bytes 2054144 | tf_op jit(solution)/shard_map/dot_general | solution.py:51
  33.7 0.0 all-reduce.2.cloned.1.call-update
  33.7 0.0 copy-done.1
  33.7 22.0 %fusion.5 = bf16[5120,256]{1,0:T(8,128)(2,1)S(1)} fusion(f32[256]{0:T(256)S(1)} %compare_select_fusion, s32[256]{0:T(256)S(1)} %copy-done.1, s32[5120]{0:T(1024)S(1)} %multiply_add_fusion), kind=kLoop, calls=%fused_computation.7 | loop fusion | flops 14417920 | bytes 2643968 | tf_op jit(solution)/shard_map/convert_element_type | solution.py:24
  55.8 35.5 %all-reduce.2.cloned.1.call-done = f32[64,256]{1,0:T(8,128)} async-done(((f32[64,256]{1,0:T(8,128)}), f32[64,256]{1,0:T(8,128)}) %all-reduce.2.cloned.1.call-update) | async-done | bytes 65552 | tf_op jit(solution)/shard_map/psum | solution.py:55
  91.3 0.8 broadcast_multiply_fusion
  92.1 9.5 %all_gather.3 = f32[256,256]{1,0:T(8,128)S(1)} all-gather(f32[64,256]{1,0:T(8,128)S(1)} %broadcast_multiply_fusion), channel_id=1, replica_groups=mesh['dp'=8,'mp'=4] {'mp'}, dimensions={0}, use_global_device_ids=true | all-gather | bytes 327680 | tf_op jit(solution)/shard_map/all_gather | solution.py:57
  101.6 1.2 select_reduce_fusion
  103.5 0.4 fusion.13
  103.9 0.4 fusion.21
  104.3 0.4 fusion.18
  104.7 0.4 fusion.39
  105.1 0.4 fusion.12
  105.5 0.4 fusion.41
  105.8 0.4 fusion.42
  106.2 0.4 fusion.11
  106.6 0.4 fusion.44
  107.0 0.4 fusion.45
  107.4 0.4 fusion.10
  107.8 0.0 copy-start
  107.8 0.4 fusion.47
  108.2 0.0 copy-start.2
  108.2 0.0 copy-start.3
  108.2 0.4 fusion.48
  108.6 0.4 fusion.9
  109.0 0.4 fusion.40
  109.4 0.4 fusion.43
  109.8 0.4 fusion.46
  110.1 0.4 fusion.49
  110.5 0.0 copy-done
  110.5 0.2 convolution_convert_fusion
  110.8 0.9 fusion.14
  111.7 0.0 copy-done.2
  111.7 0.0 copy-done.3
  111.7 23.3 %fusion = f32[1,64,5120]{2,1,0:T(8,128)} fusion(bf16[1,64,5120]{2,1,0:T(8,128)(2,1)S(1)} %copy-done.3, f32[1,64,5120]{2,1,0:T(8,128)S(1)} %copy-done.2, f32[256]{0:T(256)S(1)} %compare_select_fusion, s32[256]{0:T(256)S(1)} %copy-done.1, s32[5120]{0:T(1024)S(1)} %multiply_add_fusion, f32[64,256]{1,0:T(8,128)S(1)} %copy-done), kind=kOutput, calls=%fused_computation.2 | convolution fusion | flops 183533568 | bytes 3364864 | tf_op jit(solution)/shard_map/dot_general | solution.py:61
  (1 shorter events, 0.0 us)
Async XLA Ops:
  7.2 84.1 %all-reduce.2.cloned.1.call-start = ((), (), s32[]{:S(2)}) async-start(), calls=%async_computation | async-start | bytes 131072 | tf_op jit(solution)/shard_map/psum | solution.py:55
  7.9 25.8 %copy-start.1 = (s32[256]{0:T(256)S(1)}, s32[256]{0:T(256)}, u32[]{:S(2)}) copy-start(s32[256]{0:T(256)} %param.5) | copy-start | bytes 3076
  107.8 2.7 %copy-start = (f32[64,256]{1,0:T(8,128)S(1)}, f32[64,256]{1,0:T(8,128)}, u32[]{:S(2)}) copy-start(f32[64,256]{1,0:T(8,128)} %all-reduce.2.cloned.1.call-done) | copy-start | bytes 196612
  108.2 3.5 %copy-start.2 = (f32[1,64,5120]{2,1,0:T(8,128)S(1)}, f32[1,64,5120]{2,1,0:T(8,128)}, u32[]{:S(2)}) copy-start(f32[1,64,5120]{2,1,0:T(8,128)} %param.3) | copy-start | bytes 3932164
  108.2 3.5 %copy-start.3 = (bf16[1,64,5120]{2,1,0:T(8,128)(2,1)S(1)}, bf16[1,64,5120]{2,1,0:T(8,128)(2,1)}, u32[]{:S(2)}) copy-start(bf16[1,64,5120]{2,1,0:T(8,128)(2,1)} %param.4) | copy-start | bytes 1966084
Sparse Core Ops, SparseCore 0:
  33.8 57.4 all-reduce.1
where the time goes:
time: 142 us
  matrix products  58.3 us (41%)
  waiting for transfers between devices  35.5 us (25%)
  other arithmetic  23.6 us (17%)
  between operations  14.9 us (10%)
  blocking collectives  9.46 us (7%)
    psum x1, waiting for transfers between devices, body(): summed = lax.psum(partial_value, 'dp') / replica_count  35.5 us
    dot_general x1, matrix products, body(): jnp.dot(current.astype(jnp.bfloat16), cosines, preferred_element_type=jnp...  25.8 us
    dot_general x1, matrix products, body(): decoded = jnp.dot(coded_rows, cosines.T, preferred_element_type=jnp.float32)  23.3 us
    convert_element_type x1, other arithmetic, dct_table(): return (jnp.cos(angles) * column_scale[None, :]).astype(jnp.bfloat16)  22 us
    all_gather x1, blocking collectives, body(): block_rows = lax.all_gather(summed, 'mp', axis=0, tiled=True)  9.46 us
  transfers between devices with their start and end apart: 1, of which 1 were waited for; matrix products, arithmetic and copies ran while one was open for 16% of the time, Pallas kernels for 0%

commit v1 on v0

v1 whole, which is shorter than its diff:
```python
import functools
import math

import jax
import jax.numpy as jnp
from jax import lax
from jax.experimental import pallas as pl
from jax.experimental.pallas import tpu as pltpu
from jax.sharding import PartitionSpec as P

ITERS = 5
BLOCK = 64
CHUNK_BLOCKS = 8

inertia = 0.9
linear_term = 3.4445
cubic_term = -4.775
quintic_term = 2.0315
MESH = pl.DeviceIdType.MESH


def cos_sin(index, period):
    quarter = period // 4
    turns = jnp.floor(index * (1.0 / quarter) + 0.5)
    angle = (index - turns * quarter) * (2.0 * math.pi / period)
    quadrant = turns - 4.0 * jnp.floor(turns * 0.25)
    x2 = angle * angle
    sine = angle * (
        1.0 + x2 * (-1.0 / 6 + x2 * (1.0 / 120 + x2 * (-1.0 / 5040 + x2 * (1.0 / 362880))))
    )
    cosine = 1.0 + x2 * (
        -0.5 + x2 * (1.0 / 24 + x2 * (-1.0 / 720 + x2 * (1.0 / 40320 - x2 * (1.0 / 3628800))))
    )
    odd = (quadrant == 1.0) | (quadrant == 3.0)
    cos_part = jnp.where(odd, sine, cosine)
    sin_part = jnp.where(odd, cosine, sine)
    cos_out = jnp.where((quadrant == 1.0) | (quadrant == 2.0), -cos_part, cos_part)
    sin_out = jnp.where(quadrant >= 2.0, -sin_part, sin_part)
    return cos_out, sin_out


def split(x):
    high = x.astype(jnp.bfloat16)
    return high, (x - high.astype(jnp.float32)).astype(jnp.bfloat16)


def dot(a, b, dims=((1,), (0,))):
    return lax.dot_general(a, b, (dims, ((), ())), preferred_element_type=jnp.float32)


def dot3(a, b, dims=((1,), (0,))):
    return dot(a[0], b[0], dims) + dot(a[0], b[1], dims) + dot(a[1], b[0], dims)


def kernel(
    replicas,
    blocks,
    momentum_hbm,
    gradient_hbm,
    columns_ref,
    update_ref,
    new_hbm,
    current,
    grad,
    basis,
    cos_high,
    sin_high,
    out,
    encoded,
    swap_in,
    parts,
    full,
    load_sems,
    store_sems,
    swap_sems,
    z_send,
    z_recv,
    m_send,
    m_recv,
    f_send,
    f_recv,
):
    rows, cols = current.shape
    rank = basis.shape[1]
    half = rows // 2
    pairs = replicas // 2
    chunk = BLOCK * CHUNK_BLOCKS
    chunks = cols // chunk
    me_dp = lax.axis_index("dp")
    me_mp = lax.axis_index("mp")
    core = lax.rem(me_dp, 2)
    me_z = lax.div(me_dp, 2)
    partner = me_dp + 1 - 2 * core

    def load(step):
        span = pl.ds(pl.multiple_of(step * chunk, chunk), chunk)
        return (
            pltpu.make_async_copy(
                momentum_hbm.at[0, :, span], current.at[:, span], load_sems.at[0, step]
            ),
            pltpu.make_async_copy(
                gradient_hbm.at[0, :, span], grad.at[:, span], load_sems.at[1, step]
            ),
        )

    for step in range(chunks):
        for copy in load(step):
            copy.start()

    def z_peer(offset):
        return lax.rem(me_z + offset, pairs)

    def m_peer(offset):
        return lax.rem(me_mp + offset, blocks)

    barrier = pltpu.get_barrier_semaphore()
    pl.semaphore_signal(
        barrier, inc=1, device_id={"dp": partner, "mp": me_mp}, device_id_type=MESH
    )
    for offset in range(1, pairs):
        pl.semaphore_signal(
            barrier,
            inc=1,
            device_id={"dp": 2 * z_peer(offset) + core, "mp": me_mp},
            device_id_type=MESH,
        )
    for offset in range(1, blocks):
        pl.semaphore_signal(
            barrier,
            inc=1,
            device_id={"dp": me_dp, "mp": m_peer(offset)},
            device_id_type=MESH,
        )

    frequency = columns_ref[...].astype(jnp.float32)
    scale = jnp.where(columns_ref[...] == 0, math.sqrt(1.0 / cols), math.sqrt(2.0 / cols))
    high_count = cos_high.shape[0]
    high_index = lax.broadcasted_iota(jnp.int32, (high_count, rank), 0).astype(jnp.float32)
    ch, sh = cos_sin(high_index * frequency, 2 * cols // BLOCK)
    cos_high[...] = ch
    sin_high[...] = sh
    low_index = lax.broadcasted_iota(jnp.int32, (BLOCK, rank), 0).astype(jnp.float32)
    cl, sl = cos_sin((2.0 * low_index + 1.0) * frequency, 4 * cols)
    cl = cl * scale
    sl = sl * scale

    encoded[...] = jnp.zeros_like(encoded)

    def encode(step, carry):
        for block in range(CHUNK_BLOCKS):
            index = step * CHUNK_BLOCKS + block
            table = cos_high[pl.ds(index, 1), :] * cl - sin_high[pl.ds(index, 1), :] * sl
            start = pl.multiple_of(index * BLOCK, BLOCK)
            basis[pl.ds(start, BLOCK), :] = table.astype(jnp.bfloat16)
        for copy in load(step):
            copy.wait()
        span = pl.ds(pl.multiple_of(step * chunk, chunk), chunk)
        now = inertia * current[:, span] + grad[:, span].astype(jnp.float32)
        current[:, span] = now
        encoded[...] += dot(now.astype(jnp.bfloat16), basis[span, :])
        return carry

    lax.fori_loop(0, chunks, encode, 0)

    pl.semaphore_wait(barrier, 1 + (pairs - 1) + (blocks - 1))

    mine = pl.ds(pl.multiple_of(core * half, half), half)
    theirs = pl.ds(pl.multiple_of((1 - core) * half, half), half)
    swap = pltpu.make_async_remote_copy(
        src_ref=encoded.at[theirs, :],
        dst_ref=swap_in,
        send_sem=swap_sems.at[0],
        recv_sem=swap_sems.at[1],
        device_id={"dp": partner, "mp": me_mp},
        device_id_type=MESH,
    )
    swap.start()
    swap.wait()
    parts[me_z] = encoded[mine, :] + swap_in[...]

    z_copies = []
    for offset in range(1, pairs):
        copy = pltpu.make_async_remote_copy(
            src_ref=parts.at[me_z],
            dst_ref=parts.at[me_z],
            send_sem=z_send.at[offset],
            recv_sem=z_recv.at[offset],
            device_id={"dp": 2 * z_peer(offset) + core, "mp": me_mp},
            device_id_type=MESH,
        )
        copy.start()
        z_copies.append(copy)
    for copy in z_copies:
        copy.wait()
    total = parts[0]
    for index in range(1, pairs):
        total = total + parts[index]
    full[me_mp, core] = total * (1.0 / replicas)

    def forward(index):
        return pltpu.make_async_remote_copy(
            src_ref=full.at[index, core],
            dst_ref=full.at[index, core],
            send_sem=f_send.at[index],
            recv_sem=f_recv.at[index],
            device_id={"dp": partner, "mp": me_mp},
            device_id_type=MESH,
        )

    m_copies = []
    for offset in range(1, blocks):
        copy = pltpu.make_async_remote_copy(
            src_ref=full.at[me_mp, core],
            dst_ref=full.at[me_mp, core],
            send_sem=m_send.at[offset],
            recv_sem=m_recv.at[offset],
            device_id={"dp": me_dp, "mp": m_peer(offset)},
            device_id_type=MESH,
        )
        copy.start()
        m_copies.append(copy)
    own = forward(me_mp)
    own.start()
    own.wait()

    own_rows = full[me_mp].reshape(rows, rank)
    coded = own_rows.astype(jnp.bfloat16)

    def store(step):
        span = pl.ds(pl.multiple_of(step * chunk, chunk), chunk)
        return pltpu.make_async_copy(
            out.at[:, span], new_hbm.at[0, :, span], store_sems.at[step]
        )

    def refresh(step, carry):
        span = pl.ds(pl.multiple_of(step * chunk, chunk), chunk)
        out[:, span] = current[:, span] - dot(coded, basis[span, :], ((1,), (1,)))
        store(step).start()
        return carry

    lax.fori_loop(0, chunks, refresh, 0)

    passed = []
    for offset in range(1, blocks):
        m_copies[offset - 1].wait()
        copy = forward(lax.rem(me_mp + blocks - offset, blocks))
        copy.start()
        passed.append(copy)
    for copy in passed:
        copy.wait()

    averaged = full[...].reshape(blocks * rows, rank)
    pair = split(averaged)
    gram = dot3(pair, pair, ((0,), (0,)))
    inverse = lax.rsqrt(jnp.full((1, 1), 1e-06, jnp.float32) + jnp.sum(averaged * averaged))
    g = gram * (inverse * inverse)
    x = own_rows * inverse
    row = lax.broadcasted_iota(jnp.int32, (rank, rank), 0)
    col = lax.broadcasted_iota(jnp.int32, (rank, rank), 1)
    diagonal = jnp.where(row == col, linear_term, 0.0)
    for index in range(ITERS):
        g_pair = split(g)
        p = diagonal + cubic_term * g + quintic_term * dot3(g_pair, g_pair)
        p_pair = split(p)
        x = dot3(split(x), p_pair)
        if index < ITERS - 1:
            g = dot3(p_pair, split(dot3(p_pair, g_pair)))

    band = cols // replicas
    band_basis = basis[pl.ds(pl.multiple_of(me_dp * band, 16), band), :]
    direction = dot(x.astype(jnp.bfloat16), band_basis, ((1,), (1,)))
    update_scale = math.sqrt(rows * blocks * cols / rank)
    update_ref[...] = (direction * update_scale).astype(jnp.bfloat16)

    def drain(step, carry):
        store(step).wait()
        return carry

    lax.fori_loop(0, chunks, drain, 0)


def solution(mesh):
    replicas, blocks = mesh.shape["dp"], mesh.shape["mp"]

    def body(momentum, gradient, columns):
        _, rows, cols = momentum.shape
        rank = columns.shape[0]
        chunks = cols // (BLOCK * CHUNK_BLOCKS)
        pairs = replicas // 2
        dma = pltpu.SemaphoreType.DMA
        any_space = pl.BlockSpec(memory_space=pl.ANY)
        vmem_space = pl.BlockSpec(memory_space=pltpu.VMEM)
        return pl.pallas_call(
            functools.partial(kernel, replicas, blocks),
            out_shape=(
                jax.ShapeDtypeStruct((rows, cols // replicas), jnp.bfloat16),
                jax.ShapeDtypeStruct((1, rows, cols), jnp.float32),
            ),
            in_specs=[any_space, any_space, vmem_space],
            out_specs=(vmem_space, any_space),
            scratch_shapes=[
                pltpu.VMEM((rows, cols), jnp.float32),
                pltpu.VMEM((rows, cols), jnp.bfloat16),
                pltpu.VMEM((cols, rank), jnp.bfloat16),
                pltpu.VMEM((cols // BLOCK, rank), jnp.float32),
                pltpu.VMEM((cols // BLOCK, rank), jnp.float32),
                pltpu.VMEM((rows, cols), jnp.float32),
                pltpu.VMEM((rows, rank), jnp.float32),
                pltpu.VMEM((rows // 2, rank), jnp.float32),
                pltpu.VMEM((pairs, rows // 2, rank), jnp.float32),
                pltpu.VMEM((blocks, 2, rows // 2, rank), jnp.float32),
                dma((2, chunks)),
                dma((chunks,)),
                dma((2,)),
                dma((pairs,)),
                dma((pairs,)),
                dma((blocks,)),
                dma((blocks,)),
                dma((blocks,)),
                dma((blocks,)),
            ],
            compiler_params=pltpu.CompilerParams(collective_id=0, has_side_effects=True),
        )(momentum, gradient, columns.reshape(1, rank))

    return jax.shard_map(
        body,
        mesh=mesh,
        in_specs=(P("dp", "mp", None), P("dp", "mp", None), P()),
        out_specs=(P("mp", "dp"), P("dp", "mp", None)),
        check_vma=False,
    )
```

time: 142 us -> 29 us (0.20)
  matrix products: 58.3 us -> 0 us
  waiting for transfers between devices: 35.5 us -> 0 us
  Pallas kernels: 0 us -> 24.2 us
  other arithmetic: 23.6 us -> 0 us
  between operations: 14.9 us -> 0.64 us
  blocking collectives: 9.46 us -> 0 us
  local copies, waits for them, and re-layouts: 0.02 us -> 4 us
    dot_general x23 -> x0, matrix products: 58.3 us -> none  [the longest x1 25.8 us: body(): jnp.dot(current.astype(jnp.bfloat16), cosines, preferred_element_type=jnp...]
    psum x1 -> x0, waiting for transfers between devices: 35.5 us -> none  [body(): summed = lax.psum(partial_value, 'dp') / replica_count]
    pallas_call x0 -> x1, Pallas kernels: none -> 24.2 us  [body(): pl.pallas_call(functools.partial(kernel, replicas, blocks), out_shape=(ja...]
    convert_element_type x1 -> x0, other arithmetic: 22 us -> none  [dct_table(): return (jnp.cos(angles) * column_scale[None, :]).astype(jnp.bfloat16)]
    all_gather x1 -> x0, blocking collectives: 9.46 us -> none  [body(): block_rows = lax.all_gather(summed, 'mp', axis=0, tiled=True)]
    unnamed x8 -> x2, local copies, waits for them, and re-layouts: 0.02 us -> 4 us
  transfers between devices with their start and end apart: 1 -> 0, of which waited for: 1 -> 0; matrix products, arithmetic and copies ran while one was open for 16% -> 0% of each run, Pallas kernels for 0% -> 0%
where the time goes in v1:
time: 29 us; the launch traced here: 28.8 us
  Pallas kernels  24.2 us (83%)
  local copies, waits for them, and re-layouts  4 us (14%)
  between operations  0.64 us (2%)
    pallas_call x1, Pallas kernels, body(): pl.pallas_call(functools.partial(kernel, replicas, blocks), out_shape=(ja...  24.2 us
    unnamed x2, local copies, waits for them, and re-layouts  4 us

profile of v1, /device:TPU:0, one launch (start us, length us, event | category | flops | bytes accessed | tf_op | source)
XLA Modules:
  0.0 28.8 jit_solution(9351984564573855960)
XLA Ops:
  0.6 24.2 %shard_map.50 = (bf16[64,640]{1,0:T(8,128)(2,1)}, f32[1,64,5120]{2,1,0:T(8,128)}) custom-call(f32[1,64,5120]{2,1,0:T(8,128)} %momentum_hbm.1, bf16[1,64,5120]{2,1,0:T(8,128)(2,1)} %gradient_hbm.1, s32[1,256]{1,0:T(1,128)} %bitcast.1), custom_call_target="tpu_custom_call" | custom-call | tf_op jit(solution)/shard_map/pallas_call | solution.py:293
  24.8 1.5 %copy.7 = bf16[64,640]{1,0:T(8,128)(2,1)} copy(bf16[64,640]{1,0:T(8,128)(2,1)} %get-tuple-element.4) | data formatting | bytes 163840
  26.3 2.5 %copy.8 = f32[1,64,5120]{2,1,0:T(8,128)} copy(f32[1,64,5120]{2,1,0:T(8,128)} %get-tuple-element.5) | data formatting | bytes 2621440

commit v2 on v1

--- a/solution.py
+++ b/solution.py
@@ -16,6 +16,7 @@
 linear_term = 3.4445
 cubic_term = -4.775
 quintic_term = 2.0315
+VMEM_BYTES = 24 * 2**20
 MESH = pl.DeviceIdType.MESH
 
 
@@ -58,20 +59,17 @@
     momentum_hbm,
     gradient_hbm,
     columns_ref,
-    update_ref,
-    new_hbm,
+    full_out,
     current,
+    basis,
     grad,
-    basis,
     cos_high,
     sin_high,
-    out,
     encoded,
     swap_in,
     parts,
     full,
     load_sems,
-    store_sems,
     swap_sems,
     z_send,
     z_recv,
@@ -223,23 +221,6 @@
     own.start()
     own.wait()
 
-    own_rows = full[me_mp].reshape(rows, rank)
-    coded = own_rows.astype(jnp.bfloat16)
-
-    def store(step):
-        span = pl.ds(pl.multiple_of(step * chunk, chunk), chunk)
-        return pltpu.make_async_copy(
-            out.at[:, span], new_hbm.at[0, :, span], store_sems.at[step]
-        )
-
-    def refresh(step, carry):
-        span = pl.ds(pl.multiple_of(step * chunk, chunk), chunk)
-        out[:, span] = current[:, span] - dot(coded, basis[span, :], ((1,), (1,)))
-        store(step).start()
-        return carry
-
-    lax.fori_loop(0, chunks, refresh, 0)
-
     passed = []
     for offset in range(1, blocks):
         m_copies[offset - 1].wait()
@@ -249,7 +230,32 @@
     for copy in passed:
         copy.wait()
 
-    averaged = full[...].reshape(blocks * rows, rank)
+    full_out[...] = full[...].reshape(full_out.shape)
+
+
+def finish_kernel(
+    replicas, blocks, full_ref, current, basis, update_ref, new_hbm, out, store_sems
+):
+    rows, cols = current.shape
+    rank = basis.shape[1]
+    chunk = cols // (2 * ITERS)
+    me_dp = lax.axis_index("dp")
+    me_mp = lax.axis_index("mp")
+
+    own_rows = full_ref[pl.ds(pl.multiple_of(me_mp * rows, rows), rows), :]
+    coded = own_rows.astype(jnp.bfloat16)
+
+    def store(step):
+        span = pl.ds(step * chunk, chunk)
+        return pltpu.make_async_copy(
+            out.at[:, span], new_hbm.at[0, :, span], store_sems.at[step]
+        )
+
+    def refresh(step):
+        span = pl.ds(step * chunk, chunk)
+        out[:, span] = current[:, span] - dot(coded, basis[span, :], ((1,), (1,)))
+
+    averaged = full_ref[...]
     pair = split(averaged)
     gram = dot3(pair, pair, ((0,), (0,)))
     inverse = lax.rsqrt(jnp.full((1, 1), 1e-06, jnp.float32) + jnp.sum(averaged * averaged))
@@ -265,18 +271,18 @@
         x = dot3(split(x), p_pair)
         if index < ITERS - 1:
             g = dot3(p_pair, split(dot3(p_pair, g_pair)))
+        refresh(2 * index)
+        refresh(2 * index + 1)
+        store(2 * index).start()
+        store(2 * index + 1).start()
 
     band = cols // replicas
     band_basis = basis[pl.ds(pl.multiple_of(me_dp * band, 16), band), :]
     direction = dot(x.astype(jnp.bfloat16), band_basis, ((1,), (1,)))
     update_scale = math.sqrt(rows * blocks * cols / rank)
     update_ref[...] = (direction * update_scale).astype(jnp.bfloat16)
-
-    def drain(step, carry):
+    for step in range(2 * ITERS):
         store(step).wait()
-        return carry
-
-    lax.fori_loop(0, chunks, drain, 0)
 
 
 def solution(mesh):
@@ -288,29 +294,26 @@
         chunks = cols // (BLOCK * CHUNK_BLOCKS)
         pairs = replicas // 2
         dma = pltpu.SemaphoreType.DMA
-        any_space = pl.BlockSpec(memory_space=pl.ANY)
+        hbm_space = pl.BlockSpec(memory_space=pltpu.HBM)
         vmem_space = pl.BlockSpec(memory_space=pltpu.VMEM)
-        return pl.pallas_call(
+        full, current, basis = pl.pallas_call(
             functools.partial(kernel, replicas, blocks),
             out_shape=(
-                jax.ShapeDtypeStruct((rows, cols // replicas), jnp.bfloat16),
-                jax.ShapeDtypeStruct((1, rows, cols), jnp.float32),
-            ),
-            in_specs=[any_space, any_space, vmem_space],
-            out_specs=(vmem_space, any_space),
+                jax.ShapeDtypeStruct((blocks * rows, rank), jnp.float32),
+                jax.ShapeDtypeStruct((rows, cols), jnp.float32),
+                jax.ShapeDtypeStruct((cols, rank), jnp.bfloat16),
+            ),
+            in_specs=[hbm_space, hbm_space, vmem_space],
+            out_specs=(vmem_space, vmem_space, vmem_space),
             scratch_shapes=[
-                pltpu.VMEM((rows, cols), jnp.float32),
                 pltpu.VMEM((rows, cols), jnp.bfloat16),
-                pltpu.VMEM((cols, rank), jnp.bfloat16),
                 pltpu.VMEM((cols // BLOCK, rank), jnp.float32),
                 pltpu.VMEM((cols // BLOCK, rank), jnp.float32),
-                pltpu.VMEM((rows, cols), jnp.float32),
                 pltpu.VMEM((rows, rank), jnp.float32),
                 pltpu.VMEM((rows // 2, rank), jnp.float32),
                 pltpu.VMEM((pairs, rows // 2, rank), jnp.float32),
                 pltpu.VMEM((blocks, 2, rows // 2, rank), jnp.float32),
                 dma((2, chunks)),
-                dma((chunks,)),
                 dma((2,)),
                 dma((pairs,)),
                 dma((pairs,)),
@@ -319,8 +322,21 @@
                 dma((blocks,)),
                 dma((blocks,)),
             ],
-            compiler_params=pltpu.CompilerParams(collective_id=0, has_side_effects=True),
+            compiler_params=pltpu.CompilerParams(
+                collective_id=0, has_side_effects=True, vmem_limit_bytes=VMEM_BYTES
+            ),
         )(momentum, gradient, columns.reshape(1, rank))
+        return pl.pallas_call(
+            functools.partial(finish_kernel, replicas, blocks),
+            out_shape=(
+                jax.ShapeDtypeStruct((rows, cols // replicas), jnp.bfloat16),
+                jax.ShapeDtypeStruct((1, rows, cols), jnp.float32),
+            ),
+            in_specs=[vmem_space, vmem_space, vmem_space],
+            out_specs=(vmem_space, hbm_space),
+            scratch_shapes=[pltpu.VMEM((rows, cols), jnp.float32), dma((2 * ITERS,))],
+            compiler_params=pltpu.CompilerParams(vmem_limit_bytes=VMEM_BYTES),
+        )(full, current, basis)
 
     return jax.shard_map(
         body,

time: 29 us -> 27.9 us (0.962)
  local copies, waits for them, and re-layouts: 4 us -> 3.07 us
    pallas_call x1, Pallas kernels: 24.2 us -> 17.3 us  [body(): pl.pallas_call(functools.partial(kernel, replicas, blocks), out_shape=(ja...]
    pallas_call x0 -> x1, Pallas kernels: none -> 6.69 us  [body(): pl.pallas_call(functools.partial(finish_kernel, replicas, blocks), out_sh...]
    unnamed x2 -> x6, local copies, waits for them, and re-layouts: 4 us -> 3.07 us
where the time goes in v2:
time: 27.9 us; the launch traced here: 27.7 us
  Pallas kernels  24 us (86%)
  local copies, waits for them, and re-layouts  3.07 us (11%)
  between operations  0.65 us (2%)
    pallas_call x1, Pallas kernels, body(): pl.pallas_call(functools.partial(kernel, replicas, blocks), out_shape=(ja...  17.3 us
    pallas_call x1, Pallas kernels, body(): pl.pallas_call(functools.partial(finish_kernel, replicas, blocks), out_sh...  6.69 us
    unnamed x6, local copies, waits for them, and re-layouts  3.07 us

profile of v2, /device:TPU:0, one launch (start us, length us, event | category | flops | bytes accessed | tf_op | source)
XLA Modules:
  0.0 27.7 jit_solution(13893013846572056075)
XLA Ops:
  0.6 0.0 copy-start
  0.6 1.3 %copy-done = f32[1,64,5120]{2,1,0:T(8,128)S(1)} copy-done((f32[1,64,5120]{2,1,0:T(8,128)S(1)}, f32[1,64,5120]{2,1,0:T(8,128)}, u32[]{:S(2)}) %copy-start) | copy-done | bytes 1310744
  1.9 0.0 copy-start.1
  1.9 1.1 %copy-done.1 = bf16[1,64,5120]{2,1,0:T(8,128)(2,1)S(1)} copy-done((bf16[1,64,5120]{2,1,0:T(8,128)(2,1)S(1)}, bf16[1,64,5120]{2,1,0:T(8,128)(2,1)}, u32[]{:S(2)}) %copy-start.1) | copy-done | bytes 655384
  3.0 0.0 copy-start.2
  3.0 0.7 %copy-done.2 = s32[256]{0:T(256)S(1)} copy-done((s32[256]{0:T(256)S(1)}, s32[256]{0:T(256)}, u32[]{:S(2)}) %copy-start.2) | copy-done | bytes 1048
  3.7 17.3 %shard_map.50 = (f32[256,256]{1,0:T(8,128)S(1)}, f32[64,5120]{1,0:T(8,128)S(1)}, bf16[5120,256]{1,0:T(8,128)(2,1)S(1)}) custom-call(f32[1,64,5120]{2,1,0:T(8,128)S(1)} %copy-done, bf16[1,64,5120]{2,1,0:T(8,128)(2,1)S(1)} %copy-done.1, s32[1,256]{1,0:T(1,128)S(1)} %bitcast.1), custom_call_target="tpu_custom_call" | custom-call | tf_op jit(solution)/shard_map/pallas_call | solution.py:299
  21.0 6.7 %shard_map.51 = (bf16[64,640]{1,0:T(8,128)(2,1)}, f32[1,64,5120]{2,1,0:T(8,128)}) custom-call(f32[256,256]{1,0:T(8,128)S(1)} %get-tuple-element.5.full_ref, f32[64,5120]{1,0:T(8,128)S(1)} %get-tuple-element.6.current, bf16[5120,256]{1,0:T(8,128)(2,1)S(1)} %get-tuple-element.7.basis), custom_call_target="tpu_custom_call" | custom-call | tf_op jit(solution)/shard_map/pallas_call | solution.py:329
Async XLA Ops:
  0.6 1.3 %copy-start = (f32[1,64,5120]{2,1,0:T(8,128)S(1)}, f32[1,64,5120]{2,1,0:T(8,128)}, u32[]{:S(2)}) copy-start(f32[1,64,5120]{2,1,0:T(8,128)} %momentum_hbm.1) | copy-start | bytes 3932164
  1.9 1.1 %copy-start.1 = (bf16[1,64,5120]{2,1,0:T(8,128)(2,1)S(1)}, bf16[1,64,5120]{2,1,0:T(8,128)(2,1)}, u32[]{:S(2)}) copy-start(bf16[1,64,5120]{2,1,0:T(8,128)(2,1)} %gradient_hbm.1) | copy-start | bytes 1966084
  3.0 0.7 %copy-start.2 = (s32[256]{0:T(256)S(1)}, s32[256]{0:T(256)}, u32[]{:S(2)}) copy-start(s32[256]{0:T(256)} %param.5) | copy-start | bytes 3076

commit v3 on v2

--- a/solution.py
+++ b/solution.py
@@ -58,10 +58,11 @@
     blocks,
     momentum_hbm,
     gradient_hbm,
-    columns_ref,
+    columns_hbm,
     full_out,
     current,
     basis,
+    columns_ref,
     grad,
     cos_high,
     sin_high,
@@ -69,6 +70,7 @@
     swap_in,
     parts,
     full,
+    columns_sem,
     load_sems,
     swap_sems,
     z_send,
@@ -101,6 +103,8 @@
             ),
         )
 
+    columns_copy = pltpu.make_async_copy(columns_hbm, columns_ref, columns_sem)
+    columns_copy.start()
     for step in range(chunks):
         for copy in load(step):
             copy.start()
@@ -130,6 +134,7 @@
             device_id_type=MESH,
         )
 
+    columns_copy.wait()
     frequency = columns_ref[...].astype(jnp.float32)
     scale = jnp.where(columns_ref[...] == 0, math.sqrt(1.0 / cols), math.sqrt(2.0 / cols))
     high_count = cos_high.shape[0]
@@ -303,9 +308,10 @@
                 jax.ShapeDtypeStruct((rows, cols), jnp.float32),
                 jax.ShapeDtypeStruct((cols, rank), jnp.bfloat16),
             ),
-            in_specs=[hbm_space, hbm_space, vmem_space],
+            in_specs=[hbm_space, hbm_space, hbm_space],
             out_specs=(vmem_space, vmem_space, vmem_space),
             scratch_shapes=[
+                pltpu.VMEM((1, rank), jnp.int32),
                 pltpu.VMEM((rows, cols), jnp.bfloat16),
                 pltpu.VMEM((cols // BLOCK, rank), jnp.float32),
                 pltpu.VMEM((cols // BLOCK, rank), jnp.float32),
@@ -313,6 +319,7 @@
                 pltpu.VMEM((rows // 2, rank), jnp.float32),
                 pltpu.VMEM((pairs, rows // 2, rank), jnp.float32),
                 pltpu.VMEM((blocks, 2, rows // 2, rank), jnp.float32),
+                dma,
                 dma((2, chunks)),
                 dma((2,)),
                 dma((pairs,)),
@@ -325,7 +332,11 @@
             compiler_params=pltpu.CompilerParams(
                 collective_id=0, has_side_effects=True, vmem_limit_bytes=VMEM_BYTES
             ),
-        )(momentum, gradient, columns.reshape(1, rank))
+        )(
+            pltpu.with_memory_space_constraint(momentum, pltpu.HBM),
+            pltpu.with_memory_space_constraint(gradient, pltpu.HBM),
+            pltpu.with_memory_space_constraint(columns.reshape(1, rank), pltpu.HBM),
+        )
         return pl.pallas_call(
             functools.partial(finish_kernel, replicas, blocks),
             out_shape=(

time: 27.9 us -> 25.7 us (0.921)
  local copies, waits for them, and re-layouts: 3.07 us -> 0 us
  Pallas kernels: 24 us -> 24.9 us
    unnamed x6 -> x0, local copies, waits for them, and re-layouts: 3.07 us -> none
    pallas_call x1, Pallas kernels: 17.3 us -> 18.2 us  [body(): pl.pallas_call(functools.partial(kernel, replicas, blocks), out_shape=(ja...]
where the time goes in v3:
time: 25.7 us; the launch traced here: 25.6 us
  Pallas kernels  24.9 us (97%)
  between operations  0.64 us (2%)
    pallas_call x1, Pallas kernels, body(): pl.pallas_call(functools.partial(kernel, replicas, blocks), out_shape=(ja...  18.2 us
    pallas_call x1, Pallas kernels, body(): pl.pallas_call(functools.partial(finish_kernel, replicas, blocks), out_sh...  6.67 us

profile of v3, /device:TPU:0, one launch (start us, length us, event | category | flops | bytes accessed | tf_op | source)
XLA Modules:
  0.0 25.6 jit_solution(13230225296782264465)
XLA Ops:
  0.6 18.2 %shard_map.50 = (f32[256,256]{1,0:T(8,128)S(1)}, f32[64,5120]{1,0:T(8,128)S(1)}, bf16[5120,256]{1,0:T(8,128)(2,1)S(1)}) custom-call(f32[1,64,5120]{2,1,0:T(8,128)} %momentum_hbm.1, bf16[1,64,5120]{2,1,0:T(8,128)(2,1)} %gradient_hbm.1, s32[1,256]{1,0:T(1,128)} %bitcast.1), custom_call_target="tpu_custom_call" | custom-call | tf_op jit(solution)/shard_map/pallas_call | solution.py:304
  18.9 6.7 %shard_map.51 = (bf16[64,640]{1,0:T(8,128)(2,1)}, f32[1,64,5120]{2,1,0:T(8,128)}) custom-call(f32[256,256]{1,0:T(8,128)S(1)} %get-tuple-element.5.full_ref, f32[64,5120]{1,0:T(8,128)S(1)} %get-tuple-element.6.current, bf16[5120,256]{1,0:T(8,128)(2,1)S(1)} %get-tuple-element.7.basis), custom_call_target="tpu_custom_call" | custom-call | tf_op jit(solution)/shard_map/pallas_call | solution.py:340

commit v4 on v3

--- a/solution.py
+++ b/solution.py
@@ -16,6 +16,7 @@
 linear_term = 3.4445
 cubic_term = -4.775
 quintic_term = 2.0315
+SPLIT = 2
 VMEM_BYTES = 24 * 2**20
 MESH = pl.DeviceIdType.MESH
 
@@ -38,6 +39,17 @@
     cos_out = jnp.where((quadrant == 1.0) | (quadrant == 2.0), -cos_part, cos_part)
     sin_out = jnp.where(quadrant >= 2.0, -sin_part, sin_part)
     return cos_out, sin_out
+
+
+def peer(me, step, count, back=False):
+    if count & (count - 1):
+        return lax.rem(me + (count - step if back else step), count)
+    there, bit = me, 1
+    while bit < count:
+        if step & bit:
+            there = there + bit - 2 * bit * lax.rem(lax.div(me, bit), 2)
+        bit *= 2
+    return there
 
 
 def split(x):
@@ -109,11 +121,14 @@
         for copy in load(step):
             copy.start()
 
-    def z_peer(offset):
-        return lax.rem(me_z + offset, pairs)
-
-    def m_peer(offset):
-        return lax.rem(me_mp + offset, blocks)
+    def z_peer(step):
+        return peer(me_z, step, pairs)
+
+    def m_peer(step):
+        return peer(me_mp, step, blocks)
+
+    def m_source(step):
+        return peer(me_mp, step, blocks, back=True)
 
     barrier = pltpu.get_barrier_semaphore()
     pl.semaphore_signal(
@@ -167,74 +182,94 @@
 
     pl.semaphore_wait(barrier, 1 + (pairs - 1) + (blocks - 1))
 
-    mine = pl.ds(pl.multiple_of(core * half, half), half)
-    theirs = pl.ds(pl.multiple_of((1 - core) * half, half), half)
-    swap = pltpu.make_async_remote_copy(
-        src_ref=encoded.at[theirs, :],
-        dst_ref=swap_in,
-        send_sem=swap_sems.at[0],
-        recv_sem=swap_sems.at[1],
-        device_id={"dp": partner, "mp": me_mp},
-        device_id_type=MESH,
-    )
-    swap.start()
-    swap.wait()
-    parts[me_z] = encoded[mine, :] + swap_in[...]
+    piece = half // SPLIT
+    sends = []
+
+    def send(src, dst, send_sem, recv_sem, dp, mp):
+        copy = pltpu.make_async_remote_copy(
+            src_ref=src,
+            dst_ref=dst,
+            send_sem=send_sem,
+            recv_sem=recv_sem,
+            device_id={"dp": dp, "mp": mp},
+            device_id_type=MESH,
+        )
+        copy.start()
+        sends.append(copy)
+        return copy
+
+    def rows_of(owner, part):
+        return pl.ds(pl.multiple_of(owner * half + part * piece, piece), piece)
+
+    swaps = [
+        send(
+            encoded.at[rows_of(1 - core, part), :],
+            swap_in.at[part],
+            swap_sems.at[0, part],
+            swap_sems.at[1, part],
+            partner,
+            me_mp,
+        )
+        for part in range(SPLIT)
+    ]
 
     z_copies = []
-    for offset in range(1, pairs):
-        copy = pltpu.make_async_remote_copy(
-            src_ref=parts.at[me_z],
-            dst_ref=parts.at[me_z],
-            send_sem=z_send.at[offset],
-            recv_sem=z_recv.at[offset],
-            device_id={"dp": 2 * z_peer(offset) + core, "mp": me_mp},
-            device_id_type=MESH,
-        )
-        copy.start()
-        z_copies.append(copy)
-    for copy in z_copies:
-        copy.wait()
-    total = parts[0]
-    for index in range(1, pairs):
-        total = total + parts[index]
-    full[me_mp, core] = total * (1.0 / replicas)
-
-    def forward(index):
-        return pltpu.make_async_remote_copy(
-            src_ref=full.at[index, core],
-            dst_ref=full.at[index, core],
-            send_sem=f_send.at[index],
-            recv_sem=f_recv.at[index],
-            device_id={"dp": partner, "mp": me_mp},
-            device_id_type=MESH,
+    for part in range(SPLIT):
+        swaps[part].wait_recv()
+        parts[part, me_z] = encoded[rows_of(core, part), :] + swap_in[part]
+        z_copies.append(
+            [
+                send(
+                    parts.at[part, me_z],
+                    parts.at[part, me_z],
+                    z_send.at[part, step],
+                    z_recv.at[part, step],
+                    2 * z_peer(step) + core,
+                    me_mp,
+                )
+                for step in range(pairs - 1, 0, -1)
+            ]
+        )
+
+    passed = []
+
+    def forward(index, part):
+        place = full.at[index, core, part]
+        passed.append(
+            send(place, place, f_send.at[part, index], f_recv.at[part, index], partner, me_mp)
         )
 
     m_copies = []
-    for offset in range(1, blocks):
-        copy = pltpu.make_async_remote_copy(
-            src_ref=full.at[me_mp, core],
-            dst_ref=full.at[me_mp, core],
-            send_sem=m_send.at[offset],
-            recv_sem=m_recv.at[offset],
-            device_id={"dp": me_dp, "mp": m_peer(offset)},
-            device_id_type=MESH,
-        )
-        copy.start()
-        m_copies.append(copy)
-    own = forward(me_mp)
-    own.start()
-    own.wait()
-
-    passed = []
-    for offset in range(1, blocks):
-        m_copies[offset - 1].wait()
-        copy = forward(lax.rem(me_mp + blocks - offset, blocks))
-        copy.start()
-        passed.append(copy)
+    for part in range(SPLIT):
+        for copy in z_copies[part]:
+            copy.wait_recv()
+        total = parts[part, 0]
+        for index in range(1, pairs):
+            total = total + parts[part, index]
+        full[me_mp, core, part] = total * (1.0 / replicas)
+        place = full.at[me_mp, core, part]
+        m_copies.append(
+            [
+                send(
+                    place,
+                    place,
+                    m_send.at[part, step],
+                    m_recv.at[part, step],
+                    me_dp,
+                    m_peer(step),
+                )
+                for step in range(blocks - 1, 0, -1)
+            ]
+        )
+        forward(me_mp, part)
+    for part in range(SPLIT):
+        for step in range(1, blocks):
+            m_copies[part][blocks - 1 - step].wait_recv()
+            forward(m_source(step), part)
     for copy in passed:
-        copy.wait()
-
+        copy.wait_recv()
+    for copy in sends:
+        copy.wait_send()
     full_out[...] = full[...].reshape(full_out.shape)
 
 
@@ -298,6 +333,7 @@
         rank = columns.shape[0]
         chunks = cols // (BLOCK * CHUNK_BLOCKS)
         pairs = replicas // 2
+        piece = rows // 2 // SPLIT
         dma = pltpu.SemaphoreType.DMA
         hbm_space = pl.BlockSpec(memory_space=pltpu.HBM)
         vmem_space = pl.BlockSpec(memory_space=pltpu.VMEM)
@@ -316,18 +352,18 @@
                 pltpu.VMEM((cols // BLOCK, rank), jnp.float32),
                 pltpu.VMEM((cols // BLOCK, rank), jnp.float32),
                 pltpu.VMEM((rows, rank), jnp.float32),
-                pltpu.VMEM((rows // 2, rank), jnp.float32),
-                pltpu.VMEM((pairs, rows // 2, rank), jnp.float32),
-                pltpu.VMEM((blocks, 2, rows // 2, rank), jnp.float32),
+                pltpu.VMEM((SPLIT, piece, rank), jnp.float32),
+                pltpu.VMEM((SPLIT, pairs, piece, rank), jnp.float32),
+                pltpu.VMEM((blocks, 2, SPLIT, piece, rank), jnp.float32),
                 dma,
                 dma((2, chunks)),
-                dma((2,)),
-                dma((pairs,)),
-                dma((pairs,)),
-                dma((blocks,)),
-                dma((blocks,)),
-                dma((blocks,)),
-                dma((blocks,)),
+                dma((2, SPLIT)),
+                dma((SPLIT, pairs)),
+                dma((SPLIT, pairs)),
+                dma((SPLIT, blocks)),
+                dma((SPLIT, blocks)),
+                dma((SPLIT, blocks)),
+                dma((SPLIT, blocks)),
             ],
             compiler_params=pltpu.CompilerParams(
                 collective_id=0, has_side_effects=True, vmem_limit_bytes=VMEM_BYTES

time: 25.7 us -> 26.3 us (1.023)
  Pallas kernels: 24.9 us -> 25.5 us
    pallas_call x1, Pallas kernels: 18.2 us -> 18.8 us  [body(): pl.pallas_call(functools.partial(kernel, replicas, blocks), out_shape=(ja...]
where the time goes in v4:
time: 26.3 us; the launch traced here: 26.1 us
  Pallas kernels  25.5 us (97%)
  between operations  0.64 us (2%)
    pallas_call x1, Pallas kernels, body(): pl.pallas_call(functools.partial(kernel, replicas, blocks), out_shape=(ja...  18.8 us
    pallas_call x1, Pallas kernels, body(): pl.pallas_call(functools.partial(finish_kernel, replicas, blocks), out_sh...  6.68 us

profile of v4, /device:TPU:0, one launch (start us, length us, event | category | flops | bytes accessed | tf_op | source)
XLA Modules:
  0.0 26.1 jit_solution(6042871315313722284)
XLA Ops:
  0.6 18.8 %shard_map.50 = (f32[256,256]{1,0:T(8,128)S(1)}, f32[64,5120]{1,0:T(8,128)S(1)}, bf16[5120,256]{1,0:T(8,128)(2,1)S(1)}) custom-call(f32[1,64,5120]{2,1,0:T(8,128)} %momentum_hbm.1, bf16[1,64,5120]{2,1,0:T(8,128)(2,1)} %gradient_hbm.1, s32[1,256]{1,0:T(1,128)} %bitcast.1), custom_call_target="tpu_custom_call" | custom-call | tf_op jit(solution)/shard_map/pallas_call | solution.py:340
  19.5 6.7 %shard_map.51 = (bf16[64,640]{1,0:T(8,128)(2,1)}, f32[1,64,5120]{2,1,0:T(8,128)}) custom-call(f32[256,256]{1,0:T(8,128)S(1)} %get-tuple-element.5.full_ref, f32[64,5120]{1,0:T(8,128)S(1)} %get-tuple-element.6.current, bf16[5120,256]{1,0:T(8,128)(2,1)S(1)} %get-tuple-element.7.basis), custom_call_target="tpu_custom_call" | custom-call | tf_op jit(solution)/shard_map/pallas_call | solution.py:376

commit v5 on v3

--- a/solution.py
+++ b/solution.py
@@ -10,7 +10,7 @@
 
 ITERS = 5
 BLOCK = 64
-CHUNK_BLOCKS = 8
+CHUNK_BLOCKS = 40
 
 inertia = 0.9
 linear_term = 3.4445
@@ -50,7 +50,10 @@
 
 
 def dot3(a, b, dims=((1,), (0,))):
-    return dot(a[0], b[0], dims) + dot(a[0], b[1], dims) + dot(a[1], b[0], dims)
+    (i,), (j,) = dims
+    return dot(
+        jnp.concatenate([a[0], a[0], a[1]], axis=i), jnp.concatenate([b[0], b[1], b[0]], axis=j), dims
+    )
 
 
 def kernel(

time: 25.7 us -> 24 us (0.934)
  Pallas kernels: 24.9 us -> 23.2 us
    pallas_call x1, Pallas kernels: 18.2 us -> 16.5 us  [body(): pl.pallas_call(functools.partial(kernel, replicas, blocks), out_shape=(ja...]
where the time goes in v5:
time: 24 us; the launch traced here: 23.8 us
  Pallas kernels  23.2 us (97%)
  between operations  0.64 us (3%)
    pallas_call x1, Pallas kernels, body(): pl.pallas_call(functools.partial(kernel, replicas, blocks), out_shape=(ja...  16.5 us
    pallas_call x1, Pallas kernels, body(): pl.pallas_call(functools.partial(finish_kernel, replicas, blocks), out_sh...  6.63 us

profile of v5, /device:TPU:0, one launch (start us, length us, event | category | flops | bytes accessed | tf_op | source)
XLA Modules:
  0.0 23.8 jit_solution(7980771097484471224)
XLA Ops:
  0.6 16.5 %shard_map.50 = (f32[256,256]{1,0:T(8,128)S(1)}, f32[64,5120]{1,0:T(8,128)S(1)}, bf16[5120,256]{1,0:T(8,128)(2,1)S(1)}) custom-call(f32[1,64,5120]{2,1,0:T(8,128)} %momentum_hbm.1, bf16[1,64,5120]{2,1,0:T(8,128)(2,1)} %gradient_hbm.1, s32[1,256]{1,0:T(1,128)} %bitcast.1), custom_call_target="tpu_custom_call" | custom-call | tf_op jit(solution)/shard_map/pallas_call | solution.py:307
  17.2 6.6 %shard_map.51 = (bf16[64,640]{1,0:T(8,128)(2,1)}, f32[1,64,5120]{2,1,0:T(8,128)}) custom-call(f32[256,256]{1,0:T(8,128)S(1)} %get-tuple-element.5.full_ref, f32[64,5120]{1,0:T(8,128)S(1)} %get-tuple-element.6.current, bf16[5120,256]{1,0:T(8,128)(2,1)S(1)} %get-tuple-element.7.basis), custom_call_target="tpu_custom_call" | custom-call | tf_op jit(solution)/shard_map/pallas_call | solution.py:343

commit v6 on v5

--- a/solution.py
+++ b/solution.py
@@ -10,7 +10,7 @@
 
 ITERS = 5
 BLOCK = 64
-CHUNK_BLOCKS = 40
+CHUNK_BLOCKS = 80
 
 inertia = 0.9
 linear_term = 3.4445
@@ -263,6 +263,9 @@
         span = pl.ds(step * chunk, chunk)
         out[:, span] = current[:, span] - dot(coded, basis[span, :], ((1,), (1,)))
 
+    for step in range(2 * ITERS):
+        refresh(step)
+        store(step).start()
     averaged = full_ref[...]
     pair = split(averaged)
     gram = dot3(pair, pair, ((0,), (0,)))
@@ -279,10 +282,6 @@
         x = dot3(split(x), p_pair)
         if index < ITERS - 1:
             g = dot3(p_pair, split(dot3(p_pair, g_pair)))
-        refresh(2 * index)
-        refresh(2 * index + 1)
-        store(2 * index).start()
-        store(2 * index + 1).start()
 
     band = cols // replicas
     band_basis = basis[pl.ds(pl.multiple_of(me_dp * band, 16), band), :]

time: 24 us -> 23.8 us (level)
  no operation moved by 1% of the time
where the time goes in v6:
time: 23.8 us; the launch traced here: 23.7 us
  Pallas kernels  23 us (97%)
  between operations  0.64 us (3%)
    pallas_call x1, Pallas kernels, body(): pl.pallas_call(functools.partial(kernel, replicas, blocks), out_shape=(ja...  16.3 us
    pallas_call x1, Pallas kernels, body(): pl.pallas_call(functools.partial(finish_kernel, replicas, blocks), out_sh...  6.7 us

profile of v6, /device:TPU:0, one launch (start us, length us, event | category | flops | bytes accessed | tf_op | source)
XLA Modules:
  0.0 23.7 jit_solution(2404899132338917421)
XLA Ops:
  0.6 16.3 %shard_map.50 = (f32[256,256]{1,0:T(8,128)S(1)}, f32[64,5120]{1,0:T(8,128)S(1)}, bf16[5120,256]{1,0:T(8,128)(2,1)S(1)}) custom-call(f32[1,64,5120]{2,1,0:T(8,128)} %momentum_hbm.1, bf16[1,64,5120]{2,1,0:T(8,128)(2,1)} %gradient_hbm.1, s32[1,256]{1,0:T(1,128)} %bitcast.1), custom_call_target="tpu_custom_call" | custom-call | tf_op jit(solution)/shard_map/pallas_call | solution.py:306
  17.0 6.7 %shard_map.51 = (bf16[64,640]{1,0:T(8,128)(2,1)}, f32[1,64,5120]{2,1,0:T(8,128)}) custom-call(f32[256,256]{1,0:T(8,128)S(1)} %get-tuple-element.5.full_ref, f32[64,5120]{1,0:T(8,128)S(1)} %get-tuple-element.6.current, bf16[5120,256]{1,0:T(8,128)(2,1)S(1)} %get-tuple-element.7.basis), custom_call_target="tpu_custom_call" | custom-call | tf_op jit(solution)/shard_map/pallas_call | solution.py:342
